TPU v7x, 32 devices: a whole 2x2x4 slice. The times are simulated.
32 devices in a mesh: light: 4 (over z), pix: 4 (over x, core), cam: 2 (over y).
Axes of the slice: x: 2, y: 2, z: 4, core: 2. Of those that a mesh axis runs over, the one named last changes fastest.
Arguments:
- reflectance: bfloat16 [1024, 32, 4096], P('light', 'cam', 'pix'), may hold values from -120 to 120
- start_basis: float32 [1024, 128], replicated, may hold values from -6 to 6
Outputs:
- core_tensor: float32 [128, 32, 4096], P('light', 'cam', 'pix')
- light_basis: float32 [1024, 128], P('light')
All inputs are finite; a program needn't handle non-finite values.
Results may differ from a plain program's by a relative error of at most 0.015.
Values may be sent and summed in bfloat16 or wider, within the bound.
A program may use at most 128 MiB of HBM per device.

v0:
```python
import functools

import jax
import jax.numpy as jnp
from jax import lax
from jax.experimental import pallas as pl
from jax.experimental.pallas import tpu as pltpu
from jax.sharding import PartitionSpec as P

ITERS = 2
MESH = pl.DeviceIdType.MESH


def greet(barrier, devices):
    for device in devices:
        pl.semaphore_signal(barrier, inc=1, device_id=device, device_id_type=MESH)
    pl.semaphore_wait(barrier, len(devices))


def gather_kernel(lights, blocks, scale, source_ref, basis_ref, every_ref, image_ref, arrived, turned, tile, left, total,
                  load_sem, own_sem, tile_sem, send_sem, recv_sem, first_send, first_recv):
    me = lax.axis_index("light")
    rows, cams, width = source_ref.shape
    parts = cams // lights
    rank = image_ref.shape[1]
    height = rows // blocks
    step_rows = 16
    peers = [lax.rem(me + step, lights) for step in range(1, lights)]

    def load(block):
        return pltpu.make_async_copy(
            source_ref.at[pl.ds(block * height, height)], arrived.at[block % 2], load_sem.at[block % 2]
        )

    load(0).start()
    greet(pltpu.get_barrier_semaphore(), [{"light": peer} for peer in peers])

    def columns(part):
        return pl.ds(part * width, width)

    def first_copy(slot, peer, block):
        span = pl.ds(block * height, height)
        return pltpu.make_async_remote_copy(
            src_ref=turned.at[peer * parts, span],
            dst_ref=every_ref.at[me, span, columns(0)],
            send_sem=first_send.at[slot, block],
            recv_sem=first_recv.at[slot, block],
            device_id={"light": peer},
            device_id_type=MESH,
        )

    def later_copy(slot, peer, part):
        return pltpu.make_async_remote_copy(
            src_ref=turned.at[peer * parts + part],
            dst_ref=every_ref.at[me, :, columns(part)],
            send_sem=send_sem.at[slot, part],
            recv_sem=recv_sem.at[slot, part],
            device_id={"light": peer},
            device_id_type=MESH,
        )

    copies = [[] for _ in range(parts)]
    for block in range(blocks):
        if block + 1 < blocks:
            load(block + 1).start()
        load(block).wait()

        def turn(index, carry):
            start = pl.multiple_of(index * step_rows, step_rows)
            turned[:, pl.ds(pl.multiple_of(block * height + start, step_rows), step_rows), :] = jnp.transpose(
                arrived[block % 2, pl.ds(start, step_rows)], (1, 0, 2)
            )
            return carry

        lax.fori_loop(0, height // step_rows, turn, 0)
        for slot, peer in enumerate(peers):
            copies[0].append(first_copy(slot, peer, block))
            copies[0][-1].start()
    for part in range(1, parts):
        for slot, peer in enumerate(peers):
            copies[part].append(later_copy(slot, peer, part))
            copies[part][-1].start()
    own = [
        pltpu.make_async_copy(turned.at[me * parts + part], every_ref.at[me, :, columns(part)], own_sem.at[part])
        for part in range(parts)
    ]
    for copy in own:
        copy.start()

    basis = basis_ref[...]
    high = basis.astype(jnp.bfloat16)
    left[:rank] = high.T
    left[rank:] = (basis - high.astype(jnp.float32)).astype(jnp.bfloat16).T
    total[...] = jnp.zeros_like(total)
    chunk = 256
    for part in range(parts):
        own[part].wait()
        for copy in copies[part]:
            copy.wait_recv()
        reads = [
            pltpu.make_async_copy(
                every_ref.at[light, :, columns(part)], tile.at[pl.ds(light * rows, rows)], tile_sem.at[light]
            )
            for light in range(lights)
        ]
        for read in reads:
            read.start()
        for read in reads:
            read.wait()

        def products(index, carry):
            some = tile[:, pl.ds(pl.multiple_of(index * chunk, chunk), chunk)]
            halves = jnp.dot(left[...], some, preferred_element_type=jnp.float32)
            projected = (halves[:rank] + halves[rank:]).astype(jnp.bfloat16)
            total[...] += lax.dot_general(
                some, projected, (((1,), (1,)), ((), ())), preferred_element_type=jnp.float32
            )
            return carry

        lax.fori_loop(0, width // chunk, products, 0)
    image_ref[...] = (total[...] * scale).astype(image_ref.dtype)
    for group in copies:
        for copy in group:
            copy.wait_send()


def gather_lights(reflectance, basis, scale, collective_id):
    rows, cams, width = reflectance.shape
    lights = lax.axis_size("light")
    parts = cams // lights
    blocks = max(1, rows // 64)
    rank = basis.shape[1]
    vmem, anywhere = pl.BlockSpec(memory_space=pltpu.VMEM), pl.BlockSpec(memory_space=pl.ANY)
    dma = pltpu.SemaphoreType.DMA
    return pl.pallas_call(
        functools.partial(gather_kernel, lights, blocks, scale),
        out_shape=(
            jax.ShapeDtypeStruct((lights, rows, parts * width), reflectance.dtype),
            jax.ShapeDtypeStruct((lights * rows, rank), jnp.bfloat16),
        ),
        in_specs=[anywhere, vmem],
        out_specs=(anywhere, vmem),
        scratch_shapes=[
            pltpu.VMEM((2, rows // blocks, cams, width), reflectance.dtype),
            pltpu.VMEM((cams, rows, width), reflectance.dtype),
            pltpu.VMEM((lights * rows, width), reflectance.dtype),
            pltpu.VMEM((2 * rank, lights * rows), jnp.bfloat16),
            pltpu.VMEM((lights * rows, rank), jnp.float32),
            dma((2,)), dma((parts,)), dma((lights,)),
            dma((lights - 1, parts)), dma((lights - 1, parts)),
            dma((lights - 1, blocks)), dma((lights - 1, blocks)),
        ],
        compiler_params=pltpu.CompilerParams(
            collective_id=collective_id, has_side_effects=True, vmem_limit_bytes=40 * 1024 * 1024
        ),
    )(reflectance, basis)


def exchange_kernel(lights, src_ref, dst_ref, bounce, local_sem, send_sem, recv_sem):
    me = lax.axis_index("light")
    peers = [lax.rem(me + step, lights) for step in range(1, lights)]
    greet(pltpu.get_barrier_semaphore(), [{"light": peer} for peer in peers])
    parts, width = src_ref.shape[1], src_ref.shape[3]
    copies = []
    for part in range(parts):
        for slot, peer in enumerate(peers):
            copy = pltpu.make_async_remote_copy(
                src_ref=src_ref.at[peer, part],
                dst_ref=dst_ref.at[me, :, pl.ds(part * width, width)],
                send_sem=send_sem.at[slot, part],
                recv_sem=recv_sem.at[slot, part],
                device_id={"light": peer},
                device_id_type=MESH,
            )
            copy.start()
            copies.append(copy)
    for part in range(parts):
        inward = pltpu.make_async_copy(src_ref.at[me, part], bounce.at[part], local_sem.at[0, part])
        inward.start()
        inward.wait()
        outward = pltpu.make_async_copy(
            bounce.at[part], dst_ref.at[me, :, pl.ds(part * width, width)], local_sem.at[1, part]
        )
        outward.start()
        outward.wait()
    for copy in copies:
        copy.wait()


def exchange(blocks, collective_id):
    lights, parts, rows, width = blocks.shape
    return pl.pallas_call(
        functools.partial(exchange_kernel, lights),
        out_shape=jax.ShapeDtypeStruct((lights, rows, parts * width), blocks.dtype),
        in_specs=[pl.BlockSpec(memory_space=pl.ANY)],
        out_specs=pl.BlockSpec(memory_space=pl.ANY),
        scratch_shapes=[
            pltpu.VMEM(blocks.shape[1:], blocks.dtype),
            pltpu.SemaphoreType.DMA((2, parts)),
            pltpu.SemaphoreType.DMA((lights - 1, parts)),
            pltpu.SemaphoreType.DMA((lights - 1, parts)),
        ],
        compiler_params=pltpu.CompilerParams(
            collective_id=collective_id, has_side_effects=True, vmem_limit_bytes=8 * 1024 * 1024
        ),
    )(blocks)


def total_kernel(lights, pixes, cams, part_ref, out_ref, plane_buf, light_buf, own_buf,
                 send1, recv1, send2, recv2, send3, recv3):
    light = lax.axis_index("light")
    plane = pixes * cams
    me = lax.axis_index("pix") * cams + lax.axis_index("cam")
    rows = part_ref.shape[0] // plane

    def row_slice(index):
        return pl.ds(pl.multiple_of(index * rows, rows), rows)

    peers = [lax.rem(me + step, plane) for step in range(1, plane)]
    plane_devices = [{"pix": peer // cams, "cam": lax.rem(peer, cams)} for peer in peers]
    light_devices = [{"light": lax.rem(light + step, lights)} for step in range(1, lights)]
    greet(pltpu.get_barrier_semaphore(), plane_devices + light_devices)

    copies = []
    for slot, (peer, device) in enumerate(zip(peers, plane_devices)):
        copy = pltpu.make_async_remote_copy(
            src_ref=part_ref.at[row_slice(peer)],
            dst_ref=plane_buf.at[slot],
            send_sem=send1.at[slot],
            recv_sem=recv1.at[slot],
            device_id=device,
            device_id_type=MESH,
        )
        copy.start()
        copies.append(copy)
    total = part_ref[row_slice(me), :].astype(jnp.float32)
    for slot, copy in enumerate(copies):
        copy.wait_recv()
        total += plane_buf[slot].astype(jnp.float32)
    own_buf[...] = total.astype(own_buf.dtype)

    light_copies = []
    for slot, device in enumerate(light_devices):
        copy = pltpu.make_async_remote_copy(
            src_ref=own_buf,
            dst_ref=light_buf.at[light],
            send_sem=send2.at[slot],
            recv_sem=recv2.at[slot],
            device_id=device,
            device_id_type=MESH,
        )
        copy.start()
        light_copies.append(copy)
    light_buf[light] = own_buf[...]
    for copy in light_copies:
        copy.wait_recv()
    total = light_buf[0].astype(jnp.float32)
    for index in range(1, lights):
        total += light_buf[index].astype(jnp.float32)
    out_ref[row_slice(me), :] = total.astype(out_ref.dtype)

    last_copies = []
    for slot, device in enumerate(plane_devices):
        copy = pltpu.make_async_remote_copy(
            src_ref=out_ref.at[row_slice(me)],
            dst_ref=out_ref.at[row_slice(me)],
            send_sem=send3.at[slot],
            recv_sem=recv3.at[slot],
            device_id=device,
            device_id_type=MESH,
        )
        copy.start()
        last_copies.append(copy)
    for copy in copies + light_copies:
        copy.wait_send()
    for copy in last_copies:
        copy.wait()


def total_over_all(part, collective_id):
    lights, pixes, cams = (lax.axis_size(name) for name in ("light", "pix", "cam"))
    plane = pixes * cams
    rows = part.shape[0] // plane
    block = (rows, part.shape[1])
    dma = pltpu.SemaphoreType.DMA
    return pl.pallas_call(
        functools.partial(total_kernel, lights, pixes, cams),
        out_shape=jax.ShapeDtypeStruct(part.shape, part.dtype),
        in_specs=[pl.BlockSpec(memory_space=pltpu.VMEM)],
        out_specs=pl.BlockSpec(memory_space=pltpu.VMEM),
        scratch_shapes=[
            pltpu.VMEM((plane - 1,) + block, part.dtype),
            pltpu.VMEM((lights,) + block, part.dtype),
            pltpu.VMEM(block, part.dtype),
            dma((plane - 1,)), dma((plane - 1,)),
            dma((lights - 1,)), dma((lights - 1,)),
            dma((plane - 1,)), dma((plane - 1,)),
        ],
        compiler_params=pltpu.CompilerParams(
            collective_id=collective_id, has_side_effects=True, vmem_limit_bytes=8 * 1024 * 1024
        ),
    )(part)


def orthonormal_kernel(image_ref, basis_ref, pair_ref, whole):
    image = image_ref[...]
    rank = image.shape[1]
    inner = lax.dot_general(image, image, (((0,), (0,)), ((), ())), preferred_element_type=jnp.float32)
    height = 8
    shape = (height, rank)
    sub = lax.broadcasted_iota(jnp.int32, shape, 0)
    lane = lax.broadcasted_iota(jnp.int32, shape, 1)
    count = rank // height
    left = [inner[height * t : height * (t + 1), :] for t in range(count)]
    right = [jnp.where(lane == sub + height * t, 1.0, 0.0) for t in range(count)]

    def spread_row(tile, k):
        return jnp.broadcast_to(tile[k : k + 1, :], shape)

    def spread_column(tile, j):
        return jnp.broadcast_to(tile[:, j : j + 1], shape)

    for p in range(count):
        first = height * p
        top, below = left[p], right[p]
        columns = [spread_column(top, first + k) for k in range(height)]
        inverses, pivots = [], jnp.ones(shape, jnp.float32)
        for k in range(height):
            pivot = spread_row(columns[k], k)
            inverse = 1.0 / pivot
            pivots = jnp.where(sub == k, pivot, pivots)
            inverses.append(inverse)
            factor = jnp.where(sub > k, columns[k] * inverse, 0.0)
            for later in range(k + 1, height):
                columns[later] = columns[later] - factor * spread_row(columns[later], k)
            top = top - factor * spread_row(top, k)
            below = below - factor * spread_row(below, k)
        right[p] = below * lax.rsqrt(pivots)
        top_rows = [spread_row(top, k) * inverses[k] for k in range(height)]
        below_rows = [spread_row(below, k) * inverses[k] for k in range(height)]
        steps = [
            [spread_row(columns[later], k) * inverses[k] for later in range(k + 1, height)]
            for k in range(height)
        ]
        for t in range(p + 1, count):
            own = [spread_column(left[t], first + k) for k in range(height)]
            upper, lower = left[t], right[t]
            for k in range(height):
                for index, later in enumerate(range(k + 1, height)):
                    own[later] = own[later] - own[k] * steps[k][index]
                upper = upper - own[k] * top_rows[k]
                lower = lower - own[k] * below_rows[k]
            left[t], right[t] = upper, lower
    inverse = jnp.concatenate(right, axis=0)
    pieces = []
    for _ in range(3):
        piece = inverse.astype(jnp.bfloat16)
        pieces.append(piece)
        inverse = inverse - piece.astype(jnp.float32)
    basis = None
    for piece in reversed(pieces):
        term = lax.dot_general(
            image, piece, (((1,), (1,)), ((), ())), preferred_element_type=jnp.float32
        )
        basis = term if basis is None else basis + term
    whole[...] = basis
    own = basis_ref.shape[0]
    basis_ref[...] = whole[pl.ds(pl.multiple_of(lax.axis_index("light") * own, own), own), :]
    high = basis.astype(jnp.bfloat16)
    pair_ref[:, :rank] = high
    pair_ref[:, rank:] = (basis - high.astype(jnp.float32)).astype(jnp.bfloat16)


def orthonormal(image):
    rows, rank = image.shape
    own = rows // lax.axis_size("light")
    vmem = pl.BlockSpec(memory_space=pltpu.VMEM)
    return pl.pallas_call(
        orthonormal_kernel,
        out_shape=(
            jax.ShapeDtypeStruct((own, rank), jnp.float32),
            jax.ShapeDtypeStruct((rows, 2 * rank), jnp.bfloat16),
        ),
        in_specs=[vmem],
        out_specs=(vmem, vmem),
        scratch_shapes=[pltpu.VMEM((rows, rank), jnp.float32)],
        compiler_params=pltpu.CompilerParams(vmem_limit_bytes=16 * 1024 * 1024),
    )(image)


def per_device(reflectance, start_basis):
    light_rows, camera_cols, pixels = reflectance.shape
    rank_total = start_basis.shape[1]
    light_count = lax.axis_size("light")
    inverse_cols = 1.0 / (camera_cols * pixels * lax.axis_size("cam") * lax.axis_size("pix"))
    own_cols = camera_cols // light_count * pixels
    every_light, image_part = gather_lights(reflectance, start_basis, inverse_cols, 0)
    every_light = every_light.reshape(light_rows * light_count, own_cols)
    for iteration in range(ITERS):
        if iteration > 0:
            halves = lax.dot_general(
                pair, every_light, (((0,), (0,)), ((), ())), preferred_element_type=jnp.float32
            )
            projected = (halves[:rank_total] + halves[rank_total:]).astype(jnp.bfloat16)
            image_part = lax.dot_general(
                every_light, projected, (((1,), (1,)), ((), ())), preferred_element_type=jnp.float32
            )
            image_part = (image_part * inverse_cols).astype(jnp.bfloat16)
        basis_rows, pair = orthonormal(total_over_all(image_part, 1))
    rank_rows = rank_total // light_count
    core = lax.dot_general(
        pair[:, :rank_total], every_light, (((0,), (0,)), ((), ())),
        preferred_element_type=jnp.float32,
    ).astype(jnp.bfloat16)
    core_rows = exchange(core.reshape(light_count, 1, rank_rows, own_cols), 2)
    core_rows = core_rows.transpose(1, 0, 2).astype(jnp.float32)
    return (core_rows.reshape(rank_rows, camera_cols, pixels), basis_rows)


def solution(mesh):
    placed = (P("light", "cam", "pix"), P())
    return jax.shard_map(
        per_device,
        mesh=mesh,
        in_specs=placed,
        out_specs=(P("light", "cam", "pix"), P("light", None)),
        check_vma=False,
    )
```

profile of v0, /device:TPU:0, one launch (start us, length us, event | category | flops | bytes accessed | tf_op | source)
XLA Modules:
  0.0 267.8 jit_solution(276095898963055426)
XLA Ops:
  0.6 0.0 copy-start
  0.6 1.0 copy-done
  1.7 180.5 %shard_map.41 = (bf16[4,256,4096]{2,1,0:T(8,128)(2,1)S(1)}, bf16[1024,128]{1,0:T(8,128)(2,1)S(1)}) custom-call(bf16[256,16,1024]{2,1,0:T(8,128)(2,1)} %source_ref.1, f32[1024,128]{1,0:T(8,128)S(1)} %copy-done), custom_call_target="tpu_custom_call" | custom-call | tf_op jit(solution)/shard_map/pallas_call | solution.py:135
  182.2 25.9 %shard_map.42.image_ref = bf16[1024,128]{1,0:T(8,128)(2,1)S(1)} custom-call(bf16[1024,128]{1,0:T(8,128)(2,1)S(1)} %get-tuple-element.8.part_ref), custom_call_target="tpu_custom_call" | custom-call | tf_op jit(solution)/shard_map/pallas_call | solution.py:286
  208.1 5.9 %shard_map.43 = (f32[256,128]{1,0:T(8,128)}, bf16[1024,256]{1,0:T(8,128)(2,1)S(1)}) custom-call(bf16[1024,128]{1,0:T(8,128)(2,1)S(1)} %shard_map.42.image_ref), custom_call_target="tpu_custom_call" | custom-call | tf_op jit(solution)/shard_map/pallas_call | solution.py:378
  214.0 2.4 fusion.4
  216.4 2.3 fusion.1.part_ref
  218.7 16.1 %shard_map.44.image_ref = bf16[1024,128]{1,0:T(8,128)(2,1)S(1)} custom-call(bf16[1024,128]{1,0:T(8,128)(2,1)S(1)} %fusion.1.part_ref), custom_call_target="tpu_custom_call" | custom-call | tf_op jit(solution)/shard_map/pallas_call | solution.py:286
  234.8 6.1 %shard_map.45 = (f32[256,128]{1,0:T(8,128)}, bf16[1024,256]{1,0:T(8,128)(2,1)S(1)}) custom-call(bf16[1024,128]{1,0:T(8,128)(2,1)S(1)} %shard_map.44.image_ref), custom_call_target="tpu_custom_call" | custom-call | tf_op jit(solution)/shard_map/pallas_call | solution.py:378
  240.9 1.3 convolution_convert_fusion
  242.2 21.9 %shard_map.46 = bf16[4,32,4096]{2,1,0:T(8,128)(2,1)S(1)} custom-call(bf16[4,1,32,4096]{3,2,1,0:T(8,128)(2,1)S(1)} %bitcast.11), custom_call_target="tpu_custom_call" | custom-call | tf_op jit(solution)/shard_map/pallas_call | solution.py:192
  264.1 0.2 convert_bitcast_fusion
  264.4 1.4 copy.4
  265.7 2.1 reshape.21
Async XLA Ops:
  0.6 1.0 copy-start
where the time goes:
time: 271 us; the launch traced here: 268 us
  Pallas kernels  256 us (94%)
  matrix products  6.01 us (2%)
  local copies, waits for them, and re-layouts  4.47 us (2%)
    pallas_call x1, Pallas kernels, gather_lights(): pl.pallas_call(functools.partial(gather_kernel, lights, blocks, scale), o...  181 us
    pallas_call x2, Pallas kernels, total_over_all(): pl.pallas_call(functools.partial(total_kernel, lights, pixes, cams), out_...  42 us
    pallas_call x1, Pallas kernels, exchange(): pl.pallas_call(functools.partial(exchange_kernel, lights), out_shape=jax....  21.9 us
    pallas_call x2, Pallas kernels, orthonormal(): pl.pallas_call(orthonormal_kernel, out_shape=(jax.ShapeDtypeStruct((own,...  12 us

commit v1 on v0

v1 whole, which is shorter than its diff:
```python
import functools

import jax
import jax.numpy as jnp
from jax import lax
from jax.experimental import pallas as pl
from jax.experimental.pallas import tpu as pltpu
from jax.sharding import PartitionSpec as P

ITERS = 2
MESH = pl.DeviceIdType.MESH


def greet(barrier, devices):
    for device in devices:
        pl.semaphore_signal(barrier, inc=1, device_id=device, device_id_type=MESH)
    pl.semaphore_wait(barrier, len(devices))


def triangular_inverse(inner):
    rank = inner.shape[0]
    height = 8
    shape = (height, rank)
    sub = lax.broadcasted_iota(jnp.int32, shape, 0)
    lane = lax.broadcasted_iota(jnp.int32, shape, 1)
    count = rank // height
    left = [inner[height * t : height * (t + 1), :] for t in range(count)]
    right = [jnp.where(lane == sub + height * t, 1.0, 0.0) for t in range(count)]

    def spread_row(tile, k):
        return jnp.broadcast_to(tile[k : k + 1, :], shape)

    def spread_column(tile, j):
        return jnp.broadcast_to(tile[:, j : j + 1], shape)

    for p in range(count):
        first = height * p
        top, below = left[p], right[p]
        columns = [spread_column(top, first + k) for k in range(height)]
        inverses, pivots = [], jnp.ones(shape, jnp.float32)
        for k in range(height):
            pivot = spread_row(columns[k], k)
            inverse = 1.0 / pivot
            pivots = jnp.where(sub == k, pivot, pivots)
            inverses.append(inverse)
            factor = jnp.where(sub > k, columns[k] * inverse, 0.0)
            for later in range(k + 1, height):
                columns[later] = columns[later] - factor * spread_row(columns[later], k)
            top = top - factor * spread_row(top, k)
            below = below - factor * spread_row(below, k)
        right[p] = below * lax.rsqrt(pivots)
        top_rows = [spread_row(top, k) * inverses[k] for k in range(height)]
        below_rows = [spread_row(below, k) * inverses[k] for k in range(height)]
        steps = [
            [spread_row(columns[later], k) * inverses[k] for later in range(k + 1, height)]
            for k in range(height)
        ]
        for t in range(p + 1, count):
            own = [spread_column(left[t], first + k) for k in range(height)]
            upper, lower = left[t], right[t]
            for k in range(height):
                for index, later in enumerate(range(k + 1, height)):
                    own[later] = own[later] - own[k] * steps[k][index]
                upper = upper - own[k] * top_rows[k]
                lower = lower - own[k] * below_rows[k]
            left[t], right[t] = upper, lower
    return jnp.concatenate(right, axis=0)


def orthonormal(image):
    inner = lax.dot_general(image, image, (((0,), (0,)), ((), ())), preferred_element_type=jnp.float32)
    inverse = triangular_inverse(inner)
    pieces = []
    for _ in range(3):
        piece = inverse.astype(jnp.bfloat16)
        pieces.append(piece)
        inverse = inverse - piece.astype(jnp.float32)
    basis = None
    for piece in reversed(pieces):
        term = lax.dot_general(image, piece, (((1,), (1,)), ((), ())), preferred_element_type=jnp.float32)
        basis = term if basis is None else basis + term
    return basis


def step_kernel(lights, pixes, cams, blocks, subs, scale, source_ref, start_ref, core_ref, rows_ref,
                arrived, turned, every, left, total, gram, gram16, whole, basis16,
                part, plane_buf, own_buf, light_buf, image, ysend, yrecv,
                load_sem, own_sem, start_sem, first_send, first_recv, chunk_send, chunk_recv,
                send1, recv1, send2, recv2, send3, recv3, send4, recv4):
    light = lax.axis_index("light")
    plane = pixes * cams
    me = lax.axis_index("pix") * cams + lax.axis_index("cam")
    rows, own_cams, width = source_ref.shape
    parts = own_cams // lights
    pieces, chunks, piece = turned.shape[1], every.shape[0], every.shape[2]
    rank = rows_ref.shape[1]
    height = rows // blocks
    peers = [lax.rem(light + step, lights) for step in range(1, lights)]
    light_devices = [{"light": peer} for peer in peers]
    plane_peers = [lax.rem(me + step, plane) for step in range(1, plane)]
    plane_devices = [{"pix": peer // cams, "cam": lax.rem(peer, cams)} for peer in plane_peers]

    def load(block):
        return pltpu.make_async_copy(
            source_ref.at[pl.ds(block * height, height)], arrived.at[block % 2], load_sem.at[block % 2]
        )

    load(0).start()
    load_start = pltpu.make_async_copy(start_ref, whole, start_sem)
    load_start.start()
    greet(pltpu.get_barrier_semaphore(), plane_devices + light_devices)

    def own_rows(start, size):
        return pl.ds(pl.multiple_of(light * rows + start, 16), size)

    def first_copy(slot, block):
        return pltpu.make_async_remote_copy(
            src_ref=turned.at[peers[slot] * parts, :, pl.ds(block * height, height)],
            dst_ref=every.at[pl.ds(0, pieces), own_rows(block * height, height)],
            send_sem=first_send.at[slot, block],
            recv_sem=first_recv.at[slot, block],
            device_id=light_devices[slot],
            device_id_type=MESH,
        )

    def chunk_copy(slot, chunk):
        return pltpu.make_async_remote_copy(
            src_ref=turned.at[peers[slot] * parts + chunk // pieces, lax.rem(chunk, pieces)],
            dst_ref=every.at[chunk, own_rows(0, rows)],
            send_sem=chunk_send.at[slot, chunk - pieces],
            recv_sem=chunk_recv.at[slot, chunk - pieces],
            device_id=light_devices[slot],
            device_id_type=MESH,
        )

    def own_copy(part_index):
        return pltpu.make_async_copy(
            turned.at[light * parts + part_index],
            every.at[pl.ds(part_index * pieces, pieces), own_rows(0, rows)],
            own_sem.at[part_index],
        )

    step_rows = 16
    for block in range(blocks):
        if block + 1 < blocks:
            load(block + 1).start()
        load(block).wait()

        def turn(index, carry):
            start = pl.multiple_of(index * step_rows, step_rows)
            some = jnp.transpose(arrived[block % 2, pl.ds(start, step_rows)], (1, 0, 2))
            spot = pl.ds(pl.multiple_of(block * height + start, step_rows), step_rows)
            for q in range(pieces):
                turned[:, q, spot, :] = some[:, :, q * piece : (q + 1) * piece]
            return carry

        lax.fori_loop(0, height // step_rows, turn, 0)
        for slot in range(lights - 1):
            first_copy(slot, block).start()
    for chunk in range(pieces, chunks):
        for slot in range(lights - 1):
            chunk_copy(slot, chunk).start()
    for index in range(parts):
        own_copy(index).start()

    load_start.wait()
    basis = whole[...]
    high = basis.astype(jnp.bfloat16)
    left[:rank] = high.T
    left[rank:] = (basis - high.astype(jnp.float32)).astype(jnp.bfloat16).T
    total[...] = jnp.zeros_like(total)
    gram[...] = jnp.zeros_like(gram)
    for index in range(parts):
        own_copy(index).wait()

    def project(chunk):
        some = every[chunk]
        halves = jnp.dot(left[...], some, preferred_element_type=jnp.float32)
        projected = (halves[:rank] + halves[rank:]).astype(jnp.bfloat16)
        total[...] += lax.dot_general(
            some, projected, (((1,), (1,)), ((), ())), preferred_element_type=jnp.float32
        )

    def correlate(chunk):
        for index in range(lights):
            spot = pl.ds(index * rows, rows)
            gram[spot, :] += lax.dot_general(
                every[chunk, spot], every[chunk], (((1,), (1,)), ((), ())), preferred_element_type=jnp.float32
            )

    for slot in range(lights - 1):
        for block in range(blocks):
            first_copy(slot, block).wait_recv()

    def both(chunk, carry):
        project(chunk)
        correlate(chunk)
        return carry

    def later(chunk, carry):
        for slot in range(lights - 1):
            chunk_copy(slot, chunk).wait_recv()
        return both(chunk, carry)

    last = chunks - 1
    if chunks == pieces:
        lax.fori_loop(0, last, both, 0)
    else:
        lax.fori_loop(0, pieces, both, 0)
        lax.fori_loop(pieces, last, later, 0)
        for slot in range(lights - 1):
            chunk_copy(slot, last).wait_recv()
    project(last)

    shard = part.shape[1] // plane
    sub_rows = shard // subs

    def shard_rows(index, sub):
        return pl.ds(pl.multiple_of(index * shard + sub * sub_rows, sub_rows), sub_rows)

    def all_reduce(it, meanwhile):
        def copy1(slot, sub):
            return pltpu.make_async_remote_copy(
                src_ref=part.at[it, shard_rows(plane_peers[slot], sub)],
                dst_ref=plane_buf.at[it, slot, sub],
                send_sem=send1.at[it, slot, sub],
                recv_sem=recv1.at[it, slot, sub],
                device_id=plane_devices[slot],
                device_id_type=MESH,
            )

        def copy2(slot, sub):
            return pltpu.make_async_remote_copy(
                src_ref=own_buf.at[it, sub],
                dst_ref=light_buf.at[it, light, sub],
                send_sem=send2.at[it, slot, sub],
                recv_sem=recv2.at[it, slot, sub],
                device_id=light_devices[slot],
                device_id_type=MESH,
            )

        def copy3(slot, sub):
            return pltpu.make_async_remote_copy(
                src_ref=image.at[it, shard_rows(me, sub)],
                dst_ref=image.at[it, shard_rows(me, sub)],
                send_sem=send3.at[it, slot, sub],
                recv_sem=recv3.at[it, slot, sub],
                device_id=plane_devices[slot],
                device_id_type=MESH,
            )

        everyone, others = range(plane - 1), range(lights - 1)
        for sub in range(subs):
            for slot in everyone:
                copy1(slot, sub).start()
        meanwhile()
        for sub in range(subs):
            summed = part[it, shard_rows(me, sub), :].astype(jnp.float32)
            for slot in everyone:
                copy1(slot, sub).wait_recv()
                summed += plane_buf[it, slot, sub].astype(jnp.float32)
            own_buf[it, sub] = summed.astype(own_buf.dtype)
            for slot in others:
                copy2(slot, sub).start()
            light_buf[it, light, sub] = summed.astype(own_buf.dtype)
        for sub in range(subs):
            for slot in others:
                copy2(slot, sub).wait_recv()
            summed = light_buf[it, 0, sub].astype(jnp.float32)
            for index in range(1, lights):
                summed += light_buf[it, index, sub].astype(jnp.float32)
            image[it, shard_rows(me, sub), :] = summed.astype(image.dtype)
            for slot in everyone:
                copy3(slot, sub).start()
        for sub in range(subs):
            for slot in everyone:
                copy3(slot, sub).wait_recv()

        def finish():
            for sub in range(subs):
                for slot in everyone:
                    copy1(slot, sub).wait_send()
                    copy3(slot, sub).wait_send()
                for slot in others:
                    copy2(slot, sub).wait_send()

        return finish

    finishes = []
    for it in range(ITERS):
        if it == 0:
            part[it] = (total[...] * scale).astype(part.dtype)

            def meanwhile():
                correlate(last)
                gram16[...] = gram[...].astype(jnp.bfloat16)
        else:
            high = basis.astype(jnp.bfloat16)
            basis16[:, :rank] = high
            basis16[:, rank:] = (basis - high.astype(jnp.float32)).astype(jnp.bfloat16)
            halves = jnp.dot(gram16[...], basis16[...], preferred_element_type=jnp.float32)
            part[it] = ((halves[:, :rank] + halves[:, rank:]) * scale).astype(part.dtype)

            def meanwhile():
                pass
        finishes.append(all_reduce(it, meanwhile))
        basis = orthonormal(image[it])

    basis16[:, :rank] = basis.astype(jnp.bfloat16)
    share = rank // lights

    def copy4(slot, index):
        group = pl.ds(index * pieces, pieces)
        return pltpu.make_async_remote_copy(
            src_ref=ysend.at[peers[slot], group],
            dst_ref=yrecv.at[light, group],
            send_sem=send4.at[slot, index],
            recv_sem=recv4.at[slot, index],
            device_id=light_devices[slot],
            device_id_type=MESH,
        )

    for index in range(parts):
        for q in range(pieces):
            chunk = index * pieces + q
            y = lax.dot_general(
                basis16[:, :rank], every[chunk], (((0,), (0,)), ((), ())), preferred_element_type=jnp.float32
            ).astype(ysend.dtype)
            for k in range(lights):
                ysend[k, chunk] = y[k * share : (k + 1) * share]
        for slot in range(lights - 1):
            copy4(slot, index).start()
        yrecv[light, pl.ds(index * pieces, pieces)] = ysend[light, pl.ds(index * pieces, pieces)]
    whole[...] = basis
    rows_ref[...] = whole[own_rows(0, rows), :]
    for finish in finishes:
        finish()
    for slot in range(lights - 1):
        for block in range(blocks):
            first_copy(slot, block).wait_send()
        for chunk in range(pieces, chunks):
            chunk_copy(slot, chunk).wait_send()
    for index in range(parts):
        for slot in range(lights - 1):
            copy4(slot, index).wait_recv()
        for k in range(lights):
            for q in range(pieces):
                core_ref[:, k * parts + index, q * piece : (q + 1) * piece] = yrecv[k, index * pieces + q].astype(
                    core_ref.dtype
                )
    for index in range(parts):
        for slot in range(lights - 1):
            copy4(slot, index).wait_send()


def per_device(reflectance, start_basis):
    rows, own_cams, width = reflectance.shape
    rank = start_basis.shape[1]
    lights, pixes, cams = (lax.axis_size(name) for name in ("light", "pix", "cam"))
    plane = pixes * cams
    all_rows, share, parts = rows * lights, rank // lights, own_cams // lights
    scale = 1.0 / (own_cams * width * cams * pixes)
    piece = min(256, width)
    pieces = width // piece
    chunks = parts * pieces
    blocks = max(1, rows // 32)
    shard = all_rows // plane
    subs = 2
    vmem, anywhere = pl.BlockSpec(memory_space=pltpu.VMEM), pl.BlockSpec(memory_space=pl.ANY)
    dma = pltpu.SemaphoreType.DMA
    bf16, f32 = jnp.bfloat16, jnp.float32
    sub_shape = (subs, shard // subs, rank)
    return pl.pallas_call(
        functools.partial(step_kernel, lights, pixes, cams, blocks, subs, scale),
        out_shape=(
            jax.ShapeDtypeStruct((share, own_cams, width), f32),
            jax.ShapeDtypeStruct((rows, rank), f32),
        ),
        in_specs=[anywhere, anywhere],
        out_specs=(vmem, vmem),
        scratch_shapes=[
            pltpu.VMEM((2, rows // blocks, own_cams, width), bf16),
            pltpu.VMEM((own_cams, pieces, rows, piece), bf16),
            pltpu.VMEM((chunks, all_rows, piece), bf16),
            pltpu.VMEM((2 * rank, all_rows), bf16),
            pltpu.VMEM((all_rows, rank), f32),
            pltpu.VMEM((all_rows, all_rows), f32),
            pltpu.VMEM((all_rows, all_rows), bf16),
            pltpu.VMEM((all_rows, rank), f32),
            pltpu.VMEM((all_rows, 2 * rank), bf16),
            pltpu.VMEM((ITERS, all_rows, rank), bf16),
            pltpu.VMEM((ITERS, plane - 1) + sub_shape, bf16),
            pltpu.VMEM((ITERS,) + sub_shape, bf16),
            pltpu.VMEM((ITERS, lights) + sub_shape, bf16),
            pltpu.VMEM((ITERS, all_rows, rank), bf16),
            pltpu.VMEM((lights, chunks, share, piece), bf16),
            pltpu.VMEM((lights, chunks, share, piece), bf16),
            dma((2,)), dma((parts,)), dma,
            dma((lights - 1, blocks)), dma((lights - 1, blocks)),
            dma((lights - 1, max(1, chunks - pieces))), dma((lights - 1, max(1, chunks - pieces))),
            dma((ITERS, plane - 1, subs)), dma((ITERS, plane - 1, subs)),
            dma((ITERS, lights - 1, subs)), dma((ITERS, lights - 1, subs)),
            dma((ITERS, plane - 1, subs)), dma((ITERS, plane - 1, subs)),
            dma((lights - 1, parts)), dma((lights - 1, parts)),
        ],
        compiler_params=pltpu.CompilerParams(
            collective_id=0, has_side_effects=True, vmem_limit_bytes=60 * 1024 * 1024
        ),
    )(reflectance, start_basis)


def solution(mesh):
    return jax.shard_map(
        per_device,
        mesh=mesh,
        in_specs=(P("light", "cam", "pix"), P()),
        out_specs=(P("light", "cam", "pix"), P("light", None)),
        check_vma=False,
    )
```

time: 271 us -> 257 us (0.948); the launches traced: 268 us -> 257 us
  matrix products: 6.01 us -> 0 us
  Pallas kernels: 256 us -> 252 us
    dot_general x3 -> x0, matrix products: 6.01 us -> none  [the longest x1 2.38 us: per_device(): lax.dot_general(pair, every_light, (((0,), (0,)), ((), ())), preferred_el...]
    pallas_call x6 -> x1, Pallas kernels: 256 us -> 252 us  [per_device(): pl.pallas_call(functools.partial(step_kernel, lights, pixes, cams, blocks...]
    reshape x2 -> x0, local copies, waits for them, and re-layouts: 3.43 us -> none  [per_device(): return (core_rows.reshape(rank_rows, camera_cols, pixels), basis_rows)]
    unnamed x2 -> x4, local copies, waits for them, and re-layouts: 1.03 us -> 3.85 us
where the time goes in v1:
time: 257 us
  Pallas kernels  252 us (98%)
  local copies, waits for them, and re-layouts  3.85 us (1%)
    pallas_call x1, Pallas kernels, per_device(): pl.pallas_call(functools.partial(step_kernel, lights, pixes, cams, blocks...  252 us

profile of v1, /device:TPU:0, one launch (start us, length us, event | category | flops | bytes accessed | tf_op | source)
XLA Modules:
  0.0 256.8 jit_solution(15554477291976353325)
XLA Ops:
  0.6 252.3 %shard_map.41 = (f32[32,16,1024]{2,1,0:T(8,128)}, f32[256,128]{1,0:T(8,128)}) custom-call(bf16[256,16,1024]{2,1,0:T(8,128)(2,1)} %source_ref.1, f32[1024,128]{1,0:T(8,128)} %start_ref.1), custom_call_target="tpu_custom_call" | custom-call | tf_op jit(solution)/shard_map/pallas_call | solution.py:373
  252.9 0.0 copy-start
  252.9 3.2 %copy.6 = f32[32,16,1024]{2,1,0:T(8,128)} copy(f32[32,16,1024]{2,1,0:T(8,128)} %get-tuple-element.4) | data formatting | bytes 4194304
  256.1 0.0 copy-done
  256.1 0.7 copy.7
Async XLA Ops:
  252.9 3.2 %copy-start = (f32[256,128]{1,0:T(8,128)S(1)}, f32[256,128]{1,0:T(8,128)}, u32[]{:S(2)}) copy-start(f32[256,128]{1,0:T(8,128)} %get-tuple-element.5) | copy-start | bytes 393220

commit v2 on v1

--- a/solution.py
+++ b/solution.py
@@ -15,6 +15,17 @@
     for device in devices:
         pl.semaphore_signal(barrier, inc=1, device_id=device, device_id_type=MESH)
     pl.semaphore_wait(barrier, len(devices))
+
+
+def offsets(count):
+    even = range(0, count, 2)
+    return [(turn, swap) for turn in reversed(even) for swap in (1, 0) if turn or swap]
+
+
+def moved(place, count, offset):
+    turn, swap = offset
+    there = lax.rem(place + turn, count)
+    return there + (1 - 2 * lax.rem(there, 2)) if swap else there
 
 
 def triangular_inverse(inner):
@@ -70,35 +81,35 @@
 def orthonormal(image):
     inner = lax.dot_general(image, image, (((0,), (0,)), ((), ())), preferred_element_type=jnp.float32)
     inverse = triangular_inverse(inner)
-    pieces = []
-    for _ in range(3):
-        piece = inverse.astype(jnp.bfloat16)
-        pieces.append(piece)
-        inverse = inverse - piece.astype(jnp.float32)
-    basis = None
-    for piece in reversed(pieces):
-        term = lax.dot_general(image, piece, (((1,), (1,)), ((), ())), preferred_element_type=jnp.float32)
-        basis = term if basis is None else basis + term
-    return basis
+    high = inverse.astype(jnp.bfloat16)
+    low = (inverse - high.astype(jnp.float32)).astype(jnp.bfloat16)
+    return lax.dot_general(
+        jnp.concatenate([image, image], axis=1), jnp.concatenate([high, low], axis=1),
+        (((1,), (1,)), ((), ())), preferred_element_type=jnp.float32,
+    )
 
 
 def step_kernel(lights, pixes, cams, blocks, subs, scale, source_ref, start_ref, core_ref, rows_ref,
                 arrived, turned, every, left, total, gram, gram16, whole, basis16,
                 part, plane_buf, own_buf, light_buf, image, ysend, yrecv,
-                load_sem, own_sem, start_sem, first_send, first_recv, chunk_send, chunk_recv,
+                load_sem, own_sem, start_sem, first_send, first_recv, bulk_send, bulk_recv, chunk_send, chunk_recv,
                 send1, recv1, send2, recv2, send3, recv3, send4, recv4):
     light = lax.axis_index("light")
     plane = pixes * cams
-    me = lax.axis_index("pix") * cams + lax.axis_index("cam")
+    pix, cam = lax.axis_index("pix"), lax.axis_index("cam")
+    me = pix * cams + cam
     rows, own_cams, width = source_ref.shape
     parts = own_cams // lights
-    pieces, chunks, piece = turned.shape[1], every.shape[0], every.shape[2]
+    pieces, piece = turned.shape[1], every.shape[3]
+    others = range(lights - 1)
     rank = rows_ref.shape[1]
     height = rows // blocks
-    peers = [lax.rem(light + step, lights) for step in range(1, lights)]
+    peers = [moved(light, lights, offset) for offset in offsets(lights)]
     light_devices = [{"light": peer} for peer in peers]
-    plane_peers = [lax.rem(me + step, plane) for step in range(1, plane)]
-    plane_devices = [{"pix": peer // cams, "cam": lax.rem(peer, cams)} for peer in plane_peers]
+    steps = [(offset, turn) for offset in offsets(pixes) + [(0, 0)] for turn in range(cams) if turn or offset != (0, 0)]
+    steps.sort(key=lambda step: -(2 * (step[0][0] > 0) + 2 * (step[1] > 0) + step[0][1]))
+    plane_devices = [{"pix": moved(pix, pixes, offset), "cam": lax.rem(cam + turn, cams)} for offset, turn in steps]
+    plane_peers = [device["pix"] * cams + device["cam"] for device in plane_devices]
 
     def load(block):
         return pltpu.make_async_copy(
@@ -116,19 +127,30 @@
     def first_copy(slot, block):
         return pltpu.make_async_remote_copy(
             src_ref=turned.at[peers[slot] * parts, :, pl.ds(block * height, height)],
-            dst_ref=every.at[pl.ds(0, pieces), own_rows(block * height, height)],
+            dst_ref=every.at[0, :, own_rows(block * height, height)],
             send_sem=first_send.at[slot, block],
             recv_sem=first_recv.at[slot, block],
             device_id=light_devices[slot],
             device_id_type=MESH,
         )
 
-    def chunk_copy(slot, chunk):
+
+    def bulk_copy(slot):
         return pltpu.make_async_remote_copy(
-            src_ref=turned.at[peers[slot] * parts + chunk // pieces, lax.rem(chunk, pieces)],
-            dst_ref=every.at[chunk, own_rows(0, rows)],
-            send_sem=chunk_send.at[slot, chunk - pieces],
-            recv_sem=chunk_recv.at[slot, chunk - pieces],
+            src_ref=turned.at[pl.ds(peers[slot] * parts + 1, parts - 2)],
+            dst_ref=every.at[pl.ds(1, parts - 2), :, own_rows(0, rows)],
+            send_sem=bulk_send.at[slot],
+            recv_sem=bulk_recv.at[slot],
+            device_id=light_devices[slot],
+            device_id_type=MESH,
+        )
+
+    def chunk_copy(slot, q):
+        return pltpu.make_async_remote_copy(
+            src_ref=turned.at[peers[slot] * parts + parts - 1, q],
+            dst_ref=every.at[parts - 1, q, own_rows(0, rows)],
+            send_sem=chunk_send.at[slot, q],
+            recv_sem=chunk_recv.at[slot, q],
             device_id=light_devices[slot],
             device_id_type=MESH,
         )
@@ -136,7 +158,7 @@
     def own_copy(part_index):
         return pltpu.make_async_copy(
             turned.at[light * parts + part_index],
-            every.at[pl.ds(part_index * pieces, pieces), own_rows(0, rows)],
+            every.at[part_index, :, own_rows(0, rows)],
             own_sem.at[part_index],
         )
 
@@ -155,11 +177,14 @@
             return carry
 
         lax.fori_loop(0, height // step_rows, turn, 0)
-        for slot in range(lights - 1):
+        for slot in others:
             first_copy(slot, block).start()
-    for chunk in range(pieces, chunks):
-        for slot in range(lights - 1):
-            chunk_copy(slot, chunk).start()
+    for slot in others:
+        if parts > 2:
+            bulk_copy(slot).start()
+    for q in range(pieces if parts > 1 else 0):
+        for slot in others:
+            chunk_copy(slot, q).start()
     for index in range(parts):
         own_copy(index).start()
 
@@ -173,44 +198,42 @@
     for index in range(parts):
         own_copy(index).wait()
 
-    def project(chunk):
-        some = every[chunk]
+    def project(index, q):
+        some = every[index, q]
         halves = jnp.dot(left[...], some, preferred_element_type=jnp.float32)
         projected = (halves[:rank] + halves[rank:]).astype(jnp.bfloat16)
         total[...] += lax.dot_general(
             some, projected, (((1,), (1,)), ((), ())), preferred_element_type=jnp.float32
         )
 
-    def correlate(chunk):
-        for index in range(lights):
-            spot = pl.ds(index * rows, rows)
+    def correlate(index, q):
+        for block in range(lights):
+            spot = pl.ds(block * rows, rows)
             gram[spot, :] += lax.dot_general(
-                every[chunk, spot], every[chunk], (((1,), (1,)), ((), ())), preferred_element_type=jnp.float32
+                every[index, q, spot], every[index, q], (((1,), (1,)), ((), ())), preferred_element_type=jnp.float32
             )
 
-    for slot in range(lights - 1):
+    def both(chunk, carry):
+        index, q = chunk // pieces, lax.rem(chunk, pieces)
+        project(index, q)
+        correlate(index, q)
+        return carry
+
+    last = parts * pieces - 1
+    for slot in others:
         for block in range(blocks):
             first_copy(slot, block).wait_recv()
-
-    def both(chunk, carry):
-        project(chunk)
-        correlate(chunk)
-        return carry
-
-    def later(chunk, carry):
-        for slot in range(lights - 1):
-            chunk_copy(slot, chunk).wait_recv()
-        return both(chunk, carry)
-
-    last = chunks - 1
-    if chunks == pieces:
-        lax.fori_loop(0, last, both, 0)
-    else:
-        lax.fori_loop(0, pieces, both, 0)
-        lax.fori_loop(pieces, last, later, 0)
-        for slot in range(lights - 1):
-            chunk_copy(slot, last).wait_recv()
-    project(last)
+    lax.fori_loop(0, min(pieces, last), both, 0)
+    if parts > 2:
+        for slot in others:
+            bulk_copy(slot).wait_recv()
+        lax.fori_loop(pieces, (parts - 1) * pieces, both, 0)
+    for q in range(pieces if parts > 1 else 0):
+        for slot in others:
+            chunk_copy(slot, q).wait_recv()
+        if q < pieces - 1:
+            both((parts - 1) * pieces + q, 0)
+    project(parts - 1, pieces - 1)
 
     shard = part.shape[1] // plane
     sub_rows = shard // subs
@@ -249,7 +272,7 @@
                 device_id_type=MESH,
             )
 
-        everyone, others = range(plane - 1), range(lights - 1)
+        everyone = range(plane - 1)
         for sub in range(subs):
             for slot in everyone:
                 copy1(slot, sub).start()
@@ -292,7 +315,7 @@
             part[it] = (total[...] * scale).astype(part.dtype)
 
             def meanwhile():
-                correlate(last)
+                correlate(parts - 1, pieces - 1)
                 gram16[...] = gram[...].astype(jnp.bfloat16)
         else:
             high = basis.astype(jnp.bfloat16)
@@ -310,10 +333,9 @@
     share = rank // lights
 
     def copy4(slot, index):
-        group = pl.ds(index * pieces, pieces)
         return pltpu.make_async_remote_copy(
-            src_ref=ysend.at[peers[slot], group],
-            dst_ref=yrecv.at[light, group],
+            src_ref=ysend.at[peers[slot], index],
+            dst_ref=yrecv.at[light, index],
             send_sem=send4.at[slot, index],
             recv_sem=recv4.at[slot, index],
             device_id=light_devices[slot],
@@ -322,34 +344,35 @@
 
     for index in range(parts):
         for q in range(pieces):
-            chunk = index * pieces + q
             y = lax.dot_general(
-                basis16[:, :rank], every[chunk], (((0,), (0,)), ((), ())), preferred_element_type=jnp.float32
+                basis16[:, :rank], every[index, q], (((0,), (0,)), ((), ())), preferred_element_type=jnp.float32
             ).astype(ysend.dtype)
             for k in range(lights):
-                ysend[k, chunk] = y[k * share : (k + 1) * share]
-        for slot in range(lights - 1):
+                ysend[k, index, q] = y[k * share : (k + 1) * share]
+        for slot in others:
             copy4(slot, index).start()
-        yrecv[light, pl.ds(index * pieces, pieces)] = ysend[light, pl.ds(index * pieces, pieces)]
+        yrecv[light, index] = ysend[light, index]
     whole[...] = basis
     rows_ref[...] = whole[own_rows(0, rows), :]
     for finish in finishes:
         finish()
-    for slot in range(lights - 1):
+    for slot in others:
         for block in range(blocks):
             first_copy(slot, block).wait_send()
-        for chunk in range(pieces, chunks):
-            chunk_copy(slot, chunk).wait_send()
+        if parts > 2:
+            bulk_copy(slot).wait_send()
+        for q in range(pieces if parts > 1 else 0):
+            chunk_copy(slot, q).wait_send()
     for index in range(parts):
-        for slot in range(lights - 1):
+        for slot in others:
             copy4(slot, index).wait_recv()
         for k in range(lights):
             for q in range(pieces):
-                core_ref[:, k * parts + index, q * piece : (q + 1) * piece] = yrecv[k, index * pieces + q].astype(
+                core_ref[:, k * parts + index, q * piece : (q + 1) * piece] = yrecv[k, index, q].astype(
                     core_ref.dtype
                 )
     for index in range(parts):
-        for slot in range(lights - 1):
+        for slot in others:
             copy4(slot, index).wait_send()
 
 
@@ -362,11 +385,10 @@
     scale = 1.0 / (own_cams * width * cams * pixes)
     piece = min(256, width)
     pieces = width // piece
-    chunks = parts * pieces
-    blocks = max(1, rows // 32)
+    blocks = max(1, rows // 64)
     shard = all_rows // plane
     subs = 2
-    vmem, anywhere = pl.BlockSpec(memory_space=pltpu.VMEM), pl.BlockSpec(memory_space=pl.ANY)
+    vmem, hbm = pl.BlockSpec(memory_space=pltpu.VMEM), pl.BlockSpec(memory_space=pltpu.HBM)
     dma = pltpu.SemaphoreType.DMA
     bf16, f32 = jnp.bfloat16, jnp.float32
     sub_shape = (subs, shard // subs, rank)
@@ -376,12 +398,12 @@
             jax.ShapeDtypeStruct((share, own_cams, width), f32),
             jax.ShapeDtypeStruct((rows, rank), f32),
         ),
-        in_specs=[anywhere, anywhere],
+        in_specs=[hbm, hbm],
         out_specs=(vmem, vmem),
         scratch_shapes=[
             pltpu.VMEM((2, rows // blocks, own_cams, width), bf16),
             pltpu.VMEM((own_cams, pieces, rows, piece), bf16),
-            pltpu.VMEM((chunks, all_rows, piece), bf16),
+            pltpu.VMEM((parts, pieces, all_rows, piece), bf16),
             pltpu.VMEM((2 * rank, all_rows), bf16),
             pltpu.VMEM((all_rows, rank), f32),
             pltpu.VMEM((all_rows, all_rows), f32),
@@ -393,18 +415,18 @@
             pltpu.VMEM((ITERS,) + sub_shape, bf16),
             pltpu.VMEM((ITERS, lights) + sub_shape, bf16),
             pltpu.VMEM((ITERS, all_rows, rank), bf16),
-            pltpu.VMEM((lights, chunks, share, piece), bf16),
-            pltpu.VMEM((lights, chunks, share, piece), bf16),
+            pltpu.VMEM((lights, parts, pieces, share, piece), bf16),
+            pltpu.VMEM((lights, parts, pieces, share, piece), bf16),
             dma((2,)), dma((parts,)), dma,
             dma((lights - 1, blocks)), dma((lights - 1, blocks)),
-            dma((lights - 1, max(1, chunks - pieces))), dma((lights - 1, max(1, chunks - pieces))),
+            dma((lights - 1,)), dma((lights - 1,)), dma((lights - 1, pieces)), dma((lights - 1, pieces)),
             dma((ITERS, plane - 1, subs)), dma((ITERS, plane - 1, subs)),
             dma((ITERS, lights - 1, subs)), dma((ITERS, lights - 1, subs)),
             dma((ITERS, plane - 1, subs)), dma((ITERS, plane - 1, subs)),
             dma((lights - 1, parts)), dma((lights - 1, parts)),
         ],
         compiler_params=pltpu.CompilerParams(
-            collective_id=0, has_side_effects=True, vmem_limit_bytes=60 * 1024 * 1024
+            collective_id=0, has_side_effects=True, vmem_limit_bytes=44 * 1024 * 1024
         ),
     )(reflectance, start_basis)
 

time: 257 us -> 255 us (level)
  no operation moved by 1% of the time
where the time goes in v2:
time: 255 us
  Pallas kernels  251 us (98%)
  local copies, waits for them, and re-layouts  3.01 us (1%)
    pallas_call x1, Pallas kernels, per_device(): pl.pallas_call(functools.partial(step_kernel, lights, pixes, cams, blocks...  251 us

profile of v2, /device:TPU:0, one launch (start us, length us, event | category | flops | bytes accessed | tf_op | source)
XLA Modules:
  0.0 254.7 jit_solution(6085083957110703505)
XLA Ops:
  0.6 0.0 copy-start
  0.6 1.0 copy-done
  1.7 251.1 %shard_map.41 = (f32[32,16,1024]{2,1,0:T(8,128)S(1)}, f32[256,128]{1,0:T(8,128)S(1)}) custom-call(bf16[256,16,1024]{2,1,0:T(8,128)(2,1)} %source_ref.1, f32[1024,128]{1,0:T(8,128)S(1)} %copy-done), custom_call_target="tpu_custom_call" | custom-call | tf_op jit(solution)/shard_map/pallas_call | solution.py:395
  252.8 1.3 copy.6
  254.1 0.7 copy.7
Async XLA Ops:
  0.6 1.0 copy-start

commit v3 on v2

--- a/solution.py
+++ b/solution.py
@@ -44,36 +44,48 @@
     def spread_column(tile, j):
         return jnp.broadcast_to(tile[:, j : j + 1], shape)
 
+    columns = [spread_column(left[0], k) for k in range(height)]
     for p in range(count):
         first = height * p
-        top, below = left[p], right[p]
-        columns = [spread_column(top, first + k) for k in range(height)]
-        inverses, pivots = [], jnp.ones(shape, jnp.float32)
+        top, below, jordan = left[p], right[p], right[p]
+        ahead, own, base = [], [], []
+        if p + 1 < count:
+            ahead = [spread_column(top, first + height + k) for k in range(height)]
+            own = [spread_column(left[p + 1], first + k) for k in range(height)]
+            base = [spread_column(left[p + 1], first + height + k) for k in range(height)]
+        pivots, inverses = jnp.ones(shape, jnp.float32), jnp.ones(shape, jnp.float32)
         for k in range(height):
             pivot = spread_row(columns[k], k)
             inverse = 1.0 / pivot
             pivots = jnp.where(sub == k, pivot, pivots)
-            inverses.append(inverse)
-            factor = jnp.where(sub > k, columns[k] * inverse, 0.0)
+            inverses = jnp.where(sub == k, inverse, inverses)
+            factor = columns[k] * inverse
+            down = jnp.where(sub > k, factor, 0.0)
+            factor = jnp.where(sub != k, factor, 0.0)
             for later in range(k + 1, height):
                 columns[later] = columns[later] - factor * spread_row(columns[later], k)
+            ahead = [column - factor * spread_row(column, k) for column in ahead]
             top = top - factor * spread_row(top, k)
-            below = below - factor * spread_row(below, k)
+            jordan = jordan - factor * spread_row(jordan, k)
+            below = below - down * spread_row(below, k)
         right[p] = below * lax.rsqrt(pivots)
-        top_rows = [spread_row(top, k) * inverses[k] for k in range(height)]
-        below_rows = [spread_row(below, k) * inverses[k] for k in range(height)]
-        steps = [
-            [spread_row(columns[later], k) * inverses[k] for later in range(k + 1, height)]
-            for k in range(height)
-        ]
+        if p + 1 == count:
+            break
+        top, jordan = top * inverses, jordan * inverses
+        columns = []
+        for k in range(height):
+            scaled, column = ahead[k] * inverses, base[k]
+            for j in range(height):
+                column = column - own[j] * spread_row(scaled, j)
+            columns.append(column)
+        top_rows = [spread_row(top, k) for k in range(height)]
+        below_rows = [spread_row(jordan, k) for k in range(height)]
         for t in range(p + 1, count):
-            own = [spread_column(left[t], first + k) for k in range(height)]
+            side = own if t == p + 1 else [spread_column(left[t], first + k) for k in range(height)]
             upper, lower = left[t], right[t]
             for k in range(height):
-                for index, later in enumerate(range(k + 1, height)):
-                    own[later] = own[later] - own[k] * steps[k][index]
-                upper = upper - own[k] * top_rows[k]
-                lower = lower - own[k] * below_rows[k]
+                upper = upper - side[k] * top_rows[k]
+                lower = lower - side[k] * below_rows[k]
             left[t], right[t] = upper, lower
     return jnp.concatenate(right, axis=0)
 
@@ -177,13 +189,13 @@
             return carry
 
         lax.fori_loop(0, height // step_rows, turn, 0)
-        for slot in others:
+        for slot in reversed(others):
             first_copy(slot, block).start()
-    for slot in others:
+    for slot in reversed(others):
         if parts > 2:
             bulk_copy(slot).start()
     for q in range(pieces if parts > 1 else 0):
-        for slot in others:
+        for slot in reversed(others):
             chunk_copy(slot, q).start()
     for index in range(parts):
         own_copy(index).start()
@@ -241,7 +253,7 @@
     def shard_rows(index, sub):
         return pl.ds(pl.multiple_of(index * shard + sub * sub_rows, sub_rows), sub_rows)
 
-    def all_reduce(it, meanwhile):
+    def all_reduce(it, fill, meanwhile):
         def copy1(slot, sub):
             return pltpu.make_async_remote_copy(
                 src_ref=part.at[it, shard_rows(plane_peers[slot], sub)],
@@ -273,9 +285,11 @@
             )
 
         everyone = range(plane - 1)
-        for sub in range(subs):
-            for slot in everyone:
+        for slot in everyone:
+            fill(plane_peers[slot])
+            for sub in range(subs):
                 copy1(slot, sub).start()
+        fill(me)
         meanwhile()
         for sub in range(subs):
             summed = part[it, shard_rows(me, sub), :].astype(jnp.float32)
@@ -321,12 +335,17 @@
             high = basis.astype(jnp.bfloat16)
             basis16[:, :rank] = high
             basis16[:, rank:] = (basis - high.astype(jnp.float32)).astype(jnp.bfloat16)
-            halves = jnp.dot(gram16[...], basis16[...], preferred_element_type=jnp.float32)
-            part[it] = ((halves[:, :rank] + halves[:, rank:]) * scale).astype(part.dtype)
 
             def meanwhile():
                 pass
-        finishes.append(all_reduce(it, meanwhile))
+
+        def fill(index):
+            if it > 0:
+                spot = pl.ds(pl.multiple_of(index * shard, shard), shard)
+                halves = jnp.dot(gram16[spot, :], basis16[...], preferred_element_type=jnp.float32)
+                part[it, spot] = ((halves[:, :rank] + halves[:, rank:]) * scale).astype(part.dtype)
+
+        finishes.append(all_reduce(it, fill, meanwhile))
         basis = orthonormal(image[it])
 
     basis16[:, :rank] = basis.astype(jnp.bfloat16)
@@ -376,6 +395,29 @@
             copy4(slot, index).wait_send()
 
 
+def settle_kernel(core_ref, rows_ref, core_out, rows_out, sems):
+    copies = [
+        pltpu.make_async_copy(core_ref, core_out, sems.at[0]),
+        pltpu.make_async_copy(rows_ref, rows_out, sems.at[1]),
+    ]
+    for copy in copies:
+        copy.start()
+    for copy in copies:
+        copy.wait()
+
+
+def settle(core, rows):
+    vmem, hbm = pl.BlockSpec(memory_space=pltpu.VMEM), pl.BlockSpec(memory_space=pltpu.HBM)
+    return pl.pallas_call(
+        settle_kernel,
+        out_shape=(jax.ShapeDtypeStruct(core.shape, core.dtype), jax.ShapeDtypeStruct(rows.shape, rows.dtype)),
+        in_specs=[vmem, vmem],
+        out_specs=(hbm, hbm),
+        scratch_shapes=[pltpu.SemaphoreType.DMA((2,))],
+        compiler_params=pltpu.CompilerParams(vmem_limit_bytes=8 * 1024 * 1024),
+    )(core, rows)
+
+
 def per_device(reflectance, start_basis):
     rows, own_cams, width = reflectance.shape
     rank = start_basis.shape[1]
@@ -392,7 +434,7 @@
     dma = pltpu.SemaphoreType.DMA
     bf16, f32 = jnp.bfloat16, jnp.float32
     sub_shape = (subs, shard // subs, rank)
-    return pl.pallas_call(
+    core, basis_rows = pl.pallas_call(
         functools.partial(step_kernel, lights, pixes, cams, blocks, subs, scale),
         out_shape=(
             jax.ShapeDtypeStruct((share, own_cams, width), f32),
@@ -428,7 +470,8 @@
         compiler_params=pltpu.CompilerParams(
             collective_id=0, has_side_effects=True, vmem_limit_bytes=44 * 1024 * 1024
         ),
-    )(reflectance, start_basis)
+    )(reflectance, pltpu.with_memory_space_constraint(start_basis, pltpu.HBM))
+    return settle(core, basis_rows)
 
 
 def solution(mesh):

time: 255 us -> 251 us (0.984)
  local copies, waits for them, and re-layouts: 3.01 us -> 0 us
    unnamed x4 -> x0, local copies, waits for them, and re-layouts: 3.01 us -> none
    pallas_call x1, Pallas kernels: 251 us -> 248 us  [per_device(): pl.pallas_call(functools.partial(step_kernel, lights, pixes, cams, blocks...]
where the time goes in v3:
time: 251 us
  Pallas kernels  250 us (100%)
    pallas_call x1, Pallas kernels, per_device(): pl.pallas_call(functools.partial(step_kernel, lights, pixes, cams, blocks...  248 us

profile of v3, /device:TPU:0, one launch (start us, length us, event | category | flops | bytes accessed | tf_op | source)
XLA Modules:
  0.0 250.6 jit_solution(11465826890775200596)
XLA Ops:
  0.6 248.4 %shard_map.41 = (f32[32,16,1024]{2,1,0:T(8,128)S(1)}, f32[256,128]{1,0:T(8,128)S(1)}) custom-call(bf16[256,16,1024]{2,1,0:T(8,128)(2,1)} %source_ref.1, f32[1024,128]{1,0:T(8,128)} %start_ref.1), custom_call_target="tpu_custom_call" | custom-call | tf_op jit(solution)/shard_map/pallas_call | solution.py:437
  249.1 1.4 shard_map.42

commit v4 on v3

--- a/solution.py
+++ b/solution.py
@@ -131,7 +131,7 @@
     load(0).start()
     load_start = pltpu.make_async_copy(start_ref, whole, start_sem)
     load_start.start()
-    greet(pltpu.get_barrier_semaphore(), plane_devices + light_devices)
+    greet(pltpu.get_barrier_semaphore(), light_devices + plane_devices)
 
     def own_rows(start, size):
         return pl.ds(pl.multiple_of(light * rows + start, 16), size)
@@ -326,8 +326,6 @@
     finishes = []
     for it in range(ITERS):
         if it == 0:
-            part[it] = (total[...] * scale).astype(part.dtype)
-
             def meanwhile():
                 correlate(parts - 1, pieces - 1)
                 gram16[...] = gram[...].astype(jnp.bfloat16)
@@ -340,15 +338,17 @@
                 pass
 
         def fill(index):
-            if it > 0:
-                spot = pl.ds(pl.multiple_of(index * shard, shard), shard)
+            spot = pl.ds(pl.multiple_of(index * shard, shard), shard)
+            if it == 0:
+                part[it, spot] = (total[spot, :] * scale).astype(part.dtype)
+            else:
                 halves = jnp.dot(gram16[spot, :], basis16[...], preferred_element_type=jnp.float32)
                 part[it, spot] = ((halves[:, :rank] + halves[:, rank:]) * scale).astype(part.dtype)
 
         finishes.append(all_reduce(it, fill, meanwhile))
         basis = orthonormal(image[it])
 
-    basis16[:, :rank] = basis.astype(jnp.bfloat16)
+    left[:rank] = basis.astype(jnp.bfloat16).T
     share = rank // lights
 
     def copy4(slot, index):
@@ -363,12 +363,10 @@
 
     for index in range(parts):
         for q in range(pieces):
-            y = lax.dot_general(
-                basis16[:, :rank], every[index, q], (((0,), (0,)), ((), ())), preferred_element_type=jnp.float32
-            ).astype(ysend.dtype)
+            y = jnp.dot(left[:rank], every[index, q], preferred_element_type=jnp.float32).astype(ysend.dtype)
             for k in range(lights):
                 ysend[k, index, q] = y[k * share : (k + 1) * share]
-        for slot in others:
+        for slot in reversed(others):
             copy4(slot, index).start()
         yrecv[light, index] = ysend[light, index]
     whole[...] = basis

time: 251 us -> 250 us (level)
  no operation moved by 1% of the time
where the time goes in v4:
time: 250 us
  Pallas kernels  249 us (100%)
    pallas_call x1, Pallas kernels, per_device(): pl.pallas_call(functools.partial(step_kernel, lights, pixes, cams, blocks...  247 us

profile of v4, /device:TPU:0, one launch (start us, length us, event | category | flops | bytes accessed | tf_op | source)
XLA Modules:
  0.0 249.7 jit_solution(7975527374211619709)
XLA Ops:
  0.6 247.5 %shard_map.41 = (f32[32,16,1024]{2,1,0:T(8,128)S(1)}, f32[256,128]{1,0:T(8,128)S(1)}) custom-call(bf16[256,16,1024]{2,1,0:T(8,128)(2,1)} %source_ref.1, f32[1024,128]{1,0:T(8,128)} %start_ref.1), custom_call_target="tpu_custom_call" | custom-call | tf_op jit(solution)/shard_map/pallas_call | solution.py:435
  248.1 1.4 shard_map.42

commit v5 on v4

--- a/solution.py
+++ b/solution.py
@@ -210,12 +210,13 @@
     for index in range(parts):
         own_copy(index).wait()
 
+    def projection(index, q):
+        halves = jnp.dot(left[...], every[index, q], preferred_element_type=jnp.float32)
+        return (halves[:rank] + halves[rank:]).astype(jnp.bfloat16)
+
     def project(index, q):
-        some = every[index, q]
-        halves = jnp.dot(left[...], some, preferred_element_type=jnp.float32)
-        projected = (halves[:rank] + halves[rank:]).astype(jnp.bfloat16)
         total[...] += lax.dot_general(
-            some, projected, (((1,), (1,)), ((), ())), preferred_element_type=jnp.float32
+            every[index, q], projection(index, q), (((1,), (1,)), ((), ())), preferred_element_type=jnp.float32
         )
 
     def correlate(index, q):
@@ -245,7 +246,7 @@
             chunk_copy(slot, q).wait_recv()
         if q < pieces - 1:
             both((parts - 1) * pieces + q, 0)
-    project(parts - 1, pieces - 1)
+    projected = projection(parts - 1, pieces - 1)
 
     shard = part.shape[1] // plane
     sub_rows = shard // subs
@@ -340,7 +341,11 @@
         def fill(index):
             spot = pl.ds(pl.multiple_of(index * shard, shard), shard)
             if it == 0:
-                part[it, spot] = (total[spot, :] * scale).astype(part.dtype)
+                product = lax.dot_general(
+                    every[parts - 1, pieces - 1, spot], projected, (((1,), (1,)), ((), ())),
+                    preferred_element_type=jnp.float32,
+                )
+                part[it, spot] = ((total[spot, :] + product) * scale).astype(part.dtype)
             else:
                 halves = jnp.dot(gram16[spot, :], basis16[...], preferred_element_type=jnp.float32)
                 part[it, spot] = ((halves[:, :rank] + halves[:, rank:]) * scale).astype(part.dtype)

time: 250 us -> 249 us (level)
  no operation moved by 1% of the time
where the time goes in v5:
time: 249 us
  Pallas kernels  248 us (100%)
    pallas_call x1, Pallas kernels, per_device(): pl.pallas_call(functools.partial(step_kernel, lights, pixes, cams, blocks...  247 us

profile of v5, /device:TPU:0, one launch (start us, length us, event | category | flops | bytes accessed | tf_op | source)
XLA Modules:
  0.0 249.2 jit_solution(1988744355996120687)
XLA Ops:
  0.6 247.0 %shard_map.41 = (f32[32,16,1024]{2,1,0:T(8,128)S(1)}, f32[256,128]{1,0:T(8,128)S(1)}) custom-call(bf16[256,16,1024]{2,1,0:T(8,128)(2,1)} %source_ref.1, f32[1024,128]{1,0:T(8,128)} %start_ref.1), custom_call_target="tpu_custom_call" | custom-call | tf_op jit(solution)/shard_map/pallas_call | solution.py:440
  247.7 1.4 shard_map.42
